TPU v7x, 32 devices: a whole 2x2x4 slice. The times are simulated.
32 devices in a mesh: groups: 2 (over y), tensor: 4 (over z), dp: 4 (over x, core).
Axes of the slice: x: 2, y: 2, z: 4, core: 2. Of those that a mesh axis runs over, the one named last changes fastest.
Arguments:
- tokens: bfloat16 [256, 8192], P(('groups', 'tensor', 'dp')), parts along dimension 0, may hold values from -6 to 6
- gate_projection_matrix: bfloat16 [8192, 14336], P('dp', 'tensor'), may hold values from -0.0625 to 0.0625
- up_projection_matrix: bfloat16 [8192, 14336], P('dp', 'tensor'), may hold values from -0.0625 to 0.0625
- down_projection_matrix: bfloat16 [14336, 8192], P('tensor', 'dp'), may hold values from -0.046875 to 0.046875
- gate_adapter_inmap: bfloat16 [16384, 64], P(('groups', 'dp')), parts along dimension 0, may hold values from -0.0625 to 0.0625
- gate_adapter_outmap: bfloat16 [64, 28672], P(None, ('groups', 'tensor')), parts along dimension 1, may hold values from -0.75 to 0.75
- up_adapter_inmap: bfloat16 [16384, 64], P(('groups', 'dp')), parts along dimension 0, may hold values from -0.0625 to 0.0625
- up_adapter_outmap: bfloat16 [64, 28672], P(None, ('groups', 'tensor')), parts along dimension 1, may hold values from -0.75 to 0.75
- down_adapter_inmap: bfloat16 [28672, 64], P(('groups', 'tensor')), parts along dimension 0, may hold values from -0.046875 to 0.046875
- down_adapter_outmap: bfloat16 [64, 16384], P(None, 'groups'), parts along dimension 1, may hold values from -0.75 to 0.75
Outputs:
- block_out: bfloat16 [256, 8192], P(('groups', 'tensor', 'dp')), parts along dimension 0
There are 2 independent parts, one for each index of `groups`. A program takes and returns all parts, laid end to end along the dimension named above; an argument that names none is the same for every part. Nothing has to cross between parts.
All inputs are finite; a program needn't handle non-finite values.
Results may differ from a plain program's by a relative error of at most 0.0053.
Values may be sent and summed in bfloat16 or wider, within the bound.
A program may use at most 256 MiB of HBM per device.

v0:
```python
import jax
import jax.numpy as jnp
from jax import lax
from jax.sharding import PartitionSpec as P

adapter_scale_factor = 0.5


def body(
    tokens,
    gate_projection_matrix,
    up_projection_matrix,
    down_projection_matrix,
    gate_adapter_inmap,
    gate_adapter_outmap,
    up_adapter_inmap,
    up_adapter_outmap,
    down_adapter_inmap,
    down_adapter_outmap,
):
    tok_dev = tokens.shape[0]
    n_tensor = lax.axis_size("tensor")
    n_dp = lax.axis_size("dp")
    hidden_unit_count = gate_projection_matrix.shape[1]
    adapter_rank_size = gate_adapter_inmap.shape[1]
    columns = lax.all_to_all(tokens, "dp", split_axis=1, concat_axis=0, tiled=True)
    stacked_lowrank = jnp.concatenate(
        [gate_projection_matrix, up_projection_matrix, gate_adapter_inmap, up_adapter_inmap], axis=1
    )
    partial_all = jnp.dot(
        lax.all_gather(columns, "tensor", axis=0, tiled=True),
        stacked_lowrank,
        preferred_element_type=jnp.float32,
    )
    partial_all = partial_all.reshape(n_tensor, n_dp, tok_dev, partial_all.shape[1])
    summed_lowrank = lax.psum_scatter(partial_all, "dp", scatter_dimension=1, tiled=True)
    summed_lowrank = summed_lowrank.reshape(n_tensor * tok_dev, summed_lowrank.shape[3])
    gate_dense_part = summed_lowrank[:, :hidden_unit_count]
    up_dense_part = summed_lowrank[:, hidden_unit_count : 2 * hidden_unit_count]
    gate_lowrank_part = summed_lowrank[
        :, 2 * hidden_unit_count : 2 * hidden_unit_count + adapter_rank_size
    ].astype(jnp.bfloat16)
    up_lowrank_part = summed_lowrank[:, 2 * hidden_unit_count + adapter_rank_size :].astype(
        jnp.bfloat16
    )
    gate_activated = gate_dense_part + adapter_scale_factor * jnp.dot(
        gate_lowrank_part, gate_adapter_outmap, preferred_element_type=jnp.float32
    )
    up_projected_value = up_dense_part + adapter_scale_factor * jnp.dot(
        up_lowrank_part, up_adapter_outmap, preferred_element_type=jnp.float32
    )
    hidden_product = (jax.nn.silu(gate_activated) * up_projected_value).astype(jnp.bfloat16)
    down_outmap_single = down_adapter_outmap.astype(jnp.float32)
    lowrank_term_list = jnp.dot(
        hidden_product, down_adapter_inmap, preferred_element_type=jnp.float32
    )
    owned_lowrank_part = lax.psum_scatter(
        lowrank_term_list, "tensor", scatter_dimension=0, tiled=True
    )
    term = jnp.dot(
        hidden_product,
        lax.all_gather(down_projection_matrix, "dp", axis=1, tiled=True),
        preferred_element_type=jnp.float32,
    )
    block_result_rows = lax.psum_scatter(term, "tensor", scatter_dimension=0, tiled=True)
    block_result_rows = block_result_rows + adapter_scale_factor * jnp.dot(
        owned_lowrank_part, down_outmap_single, precision=lax.Precision.HIGHEST
    )
    return block_result_rows.astype(jnp.bfloat16)


def solution(mesh):
    placed = (
        P(("groups", "tensor", "dp"), None),
        P("dp", "tensor"),
        P("dp", "tensor"),
        P("tensor", "dp"),
        P(("groups", "dp"), None),
        P(None, ("groups", "tensor")),
        P(("groups", "dp"), None),
        P(None, ("groups", "tensor")),
        P(("groups", "tensor"), None),
        P(None, "groups"),
    )
    return jax.shard_map(
        body,
        mesh=mesh,
        in_specs=placed,
        out_specs=P(("groups", "tensor", "dp"), None),
        check_vma=False,
    )
```

profile of v0, /device:TPU:0, one launch (start us, length us, event | category | flops | bytes accessed | tf_op | source)
XLA Modules:
  0.0 576.1 jit_solution(376535880790217102)
XLA Ops:
  6.5 0.0 copy-start
  6.5 4.4 all-to-all-start
  10.9 0.0 all-reduce.4.cloned.1.call-start
  10.9 1.2 copy.13
  12.1 1.2 copy.14
  13.4 44.4 %concatenate.3 = bf16[2048,7296]{1,0:T(8,128)(2,1)} concatenate(bf16[2048,3584]{1,0:T(8,128)(2,1)} %param.11, bf16[2048,3584]{1,0:T(8,128)(2,1)} %param.12, bf16[2048,64]{1,0:T(8,128)(2,1)S(1)} %copy.13, bf16[2048,64]{1,0:T(8,128)(2,1)S(1)} %copy.14), dimensions={1} | concatenate | bytes 59768832 | tf_op jit(solution)/shard_map/concatenate | solution.py:27
  57.8 0.0 all-to-all-done
  57.8 17.1 %all_gather.6 = bf16[128,2048]{1,0:T(8,128)(2,1)S(1)} all-gather(bf16[32,2048]{1,0:T(8,128)(2,1)S(1)} %bitcast.24), channel_id=1, replica_groups=mesh['groups'=2,'tensor'=4,'dp'=4] {'tensor'}, dimensions={0}, use_global_device_ids=true | all-gather | bytes 655360 | tf_op jit(solution)/shard_map/all_gather | solution.py:31
  74.9 15.4 %fusion.13 = f32[7296,128]{0,1:T(8,128)} fusion(bf16[128,2048]{1,0:T(8,128)(2,1)S(1)} %all_gather.6, bf16[2048,7296]{1,0:T(8,128)(2,1)} %concatenate.3), kind=kOutput, calls=%fused_computation.17 | convolution fusion | flops 3825205248 | bytes 34144256 | tf_op jit(solution)/shard_map/dot_general | solution.py:30
  90.3 0.0 all-reduce.4.cloned.1.call-update
  90.3 0.0 all-gather.2.cloned.1.call-start
  90.4 0.7 all-gather.2.cloned.1.call-update
  91.1 0.0 reduce-scatter.3.cloned.1.call-start
  91.2 0.0 copy-done.5
  91.2 0.6 dynamic-slice
  91.7 78.5 %all-reduce.4.cloned.1.call-done = f32[4,4,8,7296]{3,2,1,0:T(8,128)} async-done(((f32[4,4,8,7296]{3,2,1,0:T(8,128)}), f32[4,4,8,7296]{3,2,1,0:T(8,128)}) %all-reduce.4.cloned.1.call-update) | async-done | bytes 3735568
  170.2 1.9 fusion.10
  172.2 0.0 copy-done.2
  172.2 0.2 fusion.4
  172.4 0.0 copy-done.3
  172.4 0.3 fusion.5
  172.7 0.0 copy-start.4
  172.7 0.0 copy-start.1
  172.7 345.2 %all-gather.2.cloned.1.call-done = bf16[3584,8192]{1,0:T(8,128)(2,1)} async-done(((bf16[3584,2048]{1,0:T(8,128)(2,1)}), bf16[3584,8192]{1,0:T(8,128)(2,1)}) %all-gather.2.cloned.1.call-update) | async-done | bytes 58720272 | tf_op jit(solution)/shard_map/all_gather | solution.py:62
  518.0 21.6 %fusion.11 = f32[32,8192]{1,0:T(8,128)} fusion(bf16[32,3584]{1,0:T(8,128)(2,1)S(1)} %fusion.5, bf16[3584,8192]{1,0:T(8,128)(2,1)} %all-gather.2.cloned.1.call-done), kind=kOutput, calls=%fused_computation.15 | convolution fusion | flops 1879048192 | bytes 59998208 | tf_op jit(solution)/shard_map/dot_general | solution.py:60
  539.6 0.0 reduce-scatter.3.cloned.1.call-update
  539.6 0.0 copy-done.4
  539.6 0.6 dynamic-slice.2
  540.9 0.2 fusion.12
  541.1 19.7 %all-reduce.1 = f32[32,64]{1,0:T(8,128)S(1)} all-reduce(f32[32,64]{1,0:T(8,128)S(1)} %fusion.12), channel_id=4, replica_groups=mesh['groups'=2,'tensor'=4,'dp'=4] {'tensor'}, use_global_device_ids=true, to_apply=%region_2.3.clone | all-reduce | flops 2048 | bytes 16384
  560.9 6.6 %reduce-scatter.3.cloned.1.call-done = f32[8,8192]{1,0:T(8,128)} async-done(((f32[32,8192]{1,0:T(8,128)}), f32[8,8192]{1,0:T(8,128)}) %reduce-scatter.3.cloned.1.call-update) | async-done | bytes 262160 | tf_op jit(solution)/shard_map/reduce_scatter | solution.py:65
  567.4 2.1 fusion.1
  (5 shorter events, 0.0 us)
Async XLA Ops:
  6.5 560.9 %copy-start = (bf16[64,8192]{1,0:T(8,128)(2,1)S(1)}, bf16[64,8192]{1,0:T(8,128)(2,1)}, u32[]{:S(2)}) copy-start(bf16[64,8192]{1,0:T(8,128)(2,1)} %param.19) | copy-start | bytes 3145732
  6.5 51.2 %all-to-all-start = ((bf16[8,4,2048]{2,0,1:T(8,128)(2,1)}), bf16[8,4,2048]{2,0,1:T(8,128)(2,1)S(1)}, u32[]{:S(2)}, u32[]{:S(2)}) async-start(bf16[8,4,2048]{2,0,1:T(8,128)(2,1)} %bitcast.25), calls=%async_computation | async-start | bytes 262144 | tf_op jit(solution)/shard_map/all_to_all | solution.py:26
  10.9 159.3 %all-reduce.4.cloned.1.call-start = ((), (), s32[]{:S(2)}) async-start(), calls=%async_computation.4 | async-start | bytes 7471104
  57.7 33.4 %copy-start.5 = (u32[32]{0:T(128)S(1)}, u32[32]{0:T(128)}, u32[]{:S(2)}) copy-start(u32[32]{0:T(128)} %constant.9) | copy-start | bytes 388
  57.8 114.4 %copy-start.2 = (bf16[64,3584]{1,0:T(8,128)(2,1)S(1)}, bf16[64,3584]{1,0:T(8,128)(2,1)}, u32[]{:S(2)}) copy-start(bf16[64,3584]{1,0:T(8,128)(2,1)} %param.15) | copy-start | bytes 1376260
  57.8 114.6 %copy-start.3 = (bf16[64,3584]{1,0:T(8,128)(2,1)S(1)}, bf16[64,3584]{1,0:T(8,128)(2,1)}, u32[]{:S(2)}) copy-start(bf16[64,3584]{1,0:T(8,128)(2,1)} %param.17) | copy-start | bytes 1376260
  90.3 427.6 %all-gather.2.cloned.1.call-start = ((), (), s32[]{:S(2)}) async-start(), calls=%async_computation.2 | async-start | bytes 73400320 | tf_op jit(solution)/shard_map/all_gather | solution.py:62
  91.1 476.3 %reduce-scatter.3.cloned.1.call-start = ((), (), s32[]{:S(2)}) async-start(), calls=%async_computation.3 | async-start | bytes 1310720 | tf_op jit(solution)/shard_map/reduce_scatter | solution.py:65
  172.7 366.9 %copy-start.4 = (u32[32]{0:T(128)S(1)}, u32[32]{0:T(128)}, u32[]{:S(2)}) copy-start(u32[32]{0:T(128)} %constant.13) | copy-start | bytes 388
  172.7 368.2 %copy-start.1 = (bf16[3584,64]{0,1:T(8,128)(2,1)S(1)}, bf16[3584,64]{0,1:T(8,128)(2,1)}, u32[]{:S(2)}) copy-start(bf16[3584,64]{0,1:T(8,128)(2,1)} %param.18) | copy-start | bytes 1376260
Sparse Core Ops, SparseCore 0:
  90.5 79.7 all-reduce.3
  171.8 346.1 all-gather.1
  539.8 27.6 reduce-scatter.2
where the time goes:
time: 578 us; the launch traced here: 576 us
  waiting for transfers between devices  431 us (75%)
  local copies, waits for them, and re-layouts  48 us (8%)
  matrix products  39.9 us (7%)
  blocking collectives  36.9 us (6%)
  between operations  13.9 us (2%)
    all_gather x1, waiting for transfers between devices, body(): lax.all_gather(down_projection_matrix, 'dp', axis=1, tiled=True)  345 us
    unnamed x4, waiting for transfers between devices  79.2 us
    concatenate x1, local copies, waits for them, and re-layouts, body(): jnp.concatenate([gate_projection_matrix, up_projection_matrix, gate_adapt...  44.4 us
    dot_general x1, matrix products, body(): jnp.dot(hidden_product, lax.all_gather(down_projection_matrix, 'dp', axis...  21.6 us
    unnamed x1, blocking collectives  19.7 us
    all_gather x1, blocking collectives, body(): lax.all_gather(columns, 'tensor', axis=0, tiled=True)  17.1 us
    dot_general x1, matrix products, body(): jnp.dot(lax.all_gather(columns, 'tensor', axis=0, tiled=True), stacked_lo...  15.4 us
  transfers between devices with their start and end apart: 4, of which 3 were waited for; matrix products, arithmetic and copies ran while one was open for 9% of the time, Pallas kernels for 0%

commit v1 on v0

v1 whole, which is shorter than its diff:
```python
import jax
import jax.numpy as jnp
from jax import lax
from jax.sharding import PartitionSpec as P

adapter_scale_factor = 0.5


def body(
    tokens,
    gate_projection_matrix,
    up_projection_matrix,
    down_projection_matrix,
    gate_adapter_inmap,
    gate_adapter_outmap,
    up_adapter_inmap,
    up_adapter_outmap,
    down_adapter_inmap,
    down_adapter_outmap,
):
    adapter_rank_size = gate_adapter_inmap.shape[1]
    columns = lax.all_to_all(tokens, "dp", split_axis=1, concat_axis=0, tiled=True)
    gathered = lax.all_gather(columns, "tensor", axis=0, tiled=True)

    def summed(weights):
        partial = jnp.dot(gathered, weights, preferred_element_type=jnp.float32)
        return lax.psum_scatter(partial, "dp", scatter_dimension=0, tiled=True)

    gate_dense_part = summed(gate_projection_matrix)
    up_dense_part = summed(up_projection_matrix)
    lowrank = summed(jnp.concatenate([gate_adapter_inmap, up_adapter_inmap], axis=1)).astype(
        jnp.bfloat16
    )
    gate_lowrank_part = lowrank[:, :adapter_rank_size]
    up_lowrank_part = lowrank[:, adapter_rank_size:]
    gate_activated = gate_dense_part + adapter_scale_factor * jnp.dot(
        gate_lowrank_part, gate_adapter_outmap, preferred_element_type=jnp.float32
    )
    up_projected_value = up_dense_part + adapter_scale_factor * jnp.dot(
        up_lowrank_part, up_adapter_outmap, preferred_element_type=jnp.float32
    )
    hidden_product = (jax.nn.silu(gate_activated) * up_projected_value).astype(jnp.bfloat16)
    hidden_all = lax.all_gather(hidden_product, "dp", axis=0, tiled=True)
    low = jnp.dot(hidden_all, down_adapter_inmap, preferred_element_type=jnp.float32)
    width = down_projection_matrix.shape[1]
    own_map = lax.dynamic_slice_in_dim(
        down_adapter_outmap, lax.axis_index("dp") * width, width, axis=1
    ).astype(jnp.float32)
    term = jnp.dot(hidden_all, down_projection_matrix, preferred_element_type=jnp.float32)
    term = term + adapter_scale_factor * jnp.dot(low, own_map, precision=lax.Precision.HIGHEST)
    rows_out = lax.psum_scatter(term, "tensor", scatter_dimension=0, tiled=True)
    return lax.all_to_all(
        rows_out.astype(jnp.bfloat16), "dp", split_axis=0, concat_axis=1, tiled=True
    )


def solution(mesh):
    placed = (
        P(("groups", "tensor", "dp"), None),
        P("dp", "tensor"),
        P("dp", "tensor"),
        P("tensor", "dp"),
        P(("groups", "dp"), None),
        P(None, ("groups", "tensor")),
        P(("groups", "dp"), None),
        P(None, ("groups", "tensor")),
        P(("groups", "tensor"), None),
        P(None, "groups"),
    )
    return jax.shard_map(
        body,
        mesh=mesh,
        in_specs=placed,
        out_specs=P(("groups", "tensor", "dp"), None),
        check_vma=False,
    )
```

time: 578 us -> 182 us (0.31)
  waiting for transfers between devices: 431 us -> 93.8 us
  local copies, waits for them, and re-layouts: 48 us -> 2.23 us
  matrix products: 39.9 us -> 30.4 us
    all_gather x1 -> x0, waiting for transfers between devices: 345 us -> none  [body(): lax.all_gather(down_projection_matrix, 'dp', axis=1, tiled=True)]
    reduce_scatter x1 -> x3, waiting for transfers between devices: 6.59 us -> 90.3 us  [the longest x2 62.3 us: summed(): return lax.psum_scatter(partial, 'dp', scatter_dimension=0, tiled=True)]
    unnamed x4 -> x5, waiting for transfers between devices: 79.2 us -> 3.5 us
    concatenate x1 -> x0, local copies, waits for them, and re-layouts: 44.4 us -> none  [body(): jnp.concatenate([gate_projection_matrix, up_projection_matrix, gate_adapt...]
    unnamed x1 -> x0, blocking collectives: 19.7 us -> none
    all_to_all x0 -> x2, blocking collectives: none -> 16.1 us  [the longest x1 8.97 us: body(): lax.all_to_all(tokens, 'dp', split_axis=1, concat_axis=0, tiled=True)]
    dot_general x4 -> x6, matrix products: 39.4 us -> 27.8 us  [the longest x3 18.4 us: summed(): partial = jnp.dot(gathered, weights, preferred_element_type=jnp.float32)]
    all_gather x1 -> x2, blocking collectives: 17.1 us -> 24.9 us  [the longest x1 16.2 us: body(): gathered = lax.all_gather(columns, 'tensor', axis=0, tiled=True)]
  transfers between devices with their start and end apart: 4 -> 4, of which waited for: 3 -> 4; matrix products, arithmetic and copies ran while one was open for 9% -> 11% of each run, Pallas kernels for 0% -> 0%
where the time goes in v1:
time: 182 us
  waiting for transfers between devices  93.8 us (52%)
  blocking collectives  41 us (23%)
  matrix products  30.4 us (17%)
  between operations  13.2 us (7%)
  local copies, waits for them, and re-layouts  2.23 us (1%)
    reduce_scatter x2, waiting for transfers between devices, summed(): return lax.psum_scatter(partial, 'dp', scatter_dimension=0, tiled=True)  62.3 us
    reduce_scatter x1, waiting for transfers between devices, body(): rows_out = lax.psum_scatter(term, 'tensor', scatter_dimension=0, tiled=True)  28 us
    dot_general x3, matrix products, summed(): partial = jnp.dot(gathered, weights, preferred_element_type=jnp.float32)  18.4 us
    all_gather x1, blocking collectives, body(): gathered = lax.all_gather(columns, 'tensor', axis=0, tiled=True)  16.2 us
    all_to_all x1, blocking collectives, body(): lax.all_to_all(tokens, 'dp', split_axis=1, concat_axis=0, tiled=True)  8.97 us
    all_gather x1, blocking collectives, body(): hidden_all = lax.all_gather(hidden_product, 'dp', axis=0, tiled=True)  8.74 us
    dot_general x1, matrix products, body(): jnp.dot(hidden_all, down_projection_matrix, preferred_element_type=jnp.fl...  7.51 us
    all_to_all x1, blocking collectives, body(): lax.all_to_all(rows_out.astype(jnp.bfloat16), 'dp', split_axis=0, concat_...  7.14 us
  transfers between devices with their start and end apart: 4, of which 4 were waited for; matrix products, arithmetic and copies ran while one was open for 11% of the time, Pallas kernels for 0%

profile of v1, /device:TPU:0, one launch (start us, length us, event | category | flops | bytes accessed | tf_op | source)
XLA Modules:
  0.0 181.7 jit_solution(13152078661154141634)
XLA Ops:
  6.5 0.0 copy-start
  6.5 0.0 reduce-scatter.13.cloned.1.call-start
  6.5 9.0 %all_to_all.38 = bf16[8,4,2048]{2,0,1:T(8,128)(2,1)S(1)} all-to-all(bf16[8,4,2048]{2,0,1:T(8,128)(2,1)} %bitcast.26), channel_id=1, replica_groups=mesh['groups'=2,'tensor'=4,'dp'=4] {'dp'}, dimensions={1} | all-to-all | bytes 262144 | tf_op jit(solution)/shard_map/all_to_all | solution.py:22
  15.5 16.2 %all_gather.6 = bf16[128,2048]{1,0:T(8,128)(2,1)S(1)} all-gather(bf16[32,2048]{1,0:T(8,128)(2,1)S(1)} %bitcast.24), channel_id=1, replica_groups=mesh['groups'=2,'tensor'=4,'dp'=4] {'tensor'}, dimensions={0}, use_global_device_ids=true | all-gather | bytes 655360 | tf_op jit(solution)/shard_map/all_gather | solution.py:23
  31.7 1.3 convolution_bitcast_fusion
  33.0 0.7 copy.11
  33.7 0.0 reduce-scatter.13.cloned.1.call-update
  33.8 0.0 reduce-scatter.7.cloned.1.call-start
  33.8 8.5 %fusion.13 = f32[128,3584]{1,0:T(8,128)} fusion(bf16[128,2048]{1,0:T(8,128)(2,1)S(1)} %all_gather.6, bf16[2048,3584]{1,0:T(8,128)(2,1)} %param.11), kind=kOutput, calls=%fused_computation.18 | convolution fusion | flops 1879048192 | bytes 17039360 | tf_op jit(solution)/shard_map/dot_general | solution.py:26
  42.3 0.0 reduce-scatter.7.cloned.1.call-update
  42.3 0.0 reduce-scatter.9.cloned.1.call-start
  42.4 8.6 %fusion.14 = f32[128,3584]{1,0:T(8,128)} fusion(bf16[128,2048]{1,0:T(8,128)(2,1)S(1)} %all_gather.6, bf16[2048,3584]{1,0:T(8,128)(2,1)} %param.12), kind=kOutput, calls=%fused_computation.19 | convolution fusion | flops 1879048192 | bytes 17039360 | tf_op jit(solution)/shard_map/dot_general | solution.py:26
  51.0 0.0 reduce-scatter.9.cloned.1.call-update
  51.0 0.0 reduce-scatter.11.cloned.1.call-start
  51.1 3.4 %reduce-scatter.13.cloned.1.call-done = f32[32,128]{1,0:T(8,128)} async-done(((f32[128,128]{1,0:T(8,128)}), f32[32,128]{1,0:T(8,128)}) %reduce-scatter.13.cloned.1.call-update) | async-done | bytes 16400
  54.5 0.8 copy.12
  55.3 31.4 %reduce-scatter.7.cloned.1.call-done = f32[32,3584]{1,0:T(8,128)} async-done(((f32[128,3584]{1,0:T(8,128)}), f32[32,3584]{1,0:T(8,128)}) %reduce-scatter.7.cloned.1.call-update) | async-done | bytes 458768 | tf_op jit(solution)/shard_map/reduce_scatter | solution.py:27
  86.7 0.0 copy-done.2
  86.7 1.3 fusion.2
  88.0 30.9 %reduce-scatter.9.cloned.1.call-done = f32[32,3584]{1,0:T(8,128)} async-done(((f32[128,3584]{1,0:T(8,128)}), f32[32,3584]{1,0:T(8,128)}) %reduce-scatter.9.cloned.1.call-update) | async-done | bytes 458768 | tf_op jit(solution)/shard_map/reduce_scatter | solution.py:27
  118.9 0.0 copy-done.3
  118.9 1.3 fusion.3
  120.2 8.7 %all_gather.7 = bf16[128,3584]{1,0:T(8,128)(2,1)S(1)} all-gather(bf16[32,3584]{1,0:T(8,128)(2,1)S(1)} %fusion.3), channel_id=1, replica_groups=mesh['groups'=2,'tensor'=4,'dp'=4] {'dp'}, dimensions={0}, use_global_device_ids=true | all-gather | bytes 1146880 | tf_op jit(solution)/shard_map/all_gather | solution.py:43
  128.9 7.5 %fusion.15 = f32[128,2048]{1,0:T(8,128)S(1)} fusion(bf16[128,3584]{1,0:T(8,128)(2,1)S(1)} %all_gather.7, bf16[3584,2048]{1,0:T(8,128)(2,1)} %param.13), kind=kOutput, calls=%fused_computation.20 | convolution fusion | flops 1879048192 | bytes 16646144 | tf_op jit(solution)/shard_map/dot_general | solution.py:49
  136.4 0.0 copy-done.1
  136.4 0.4 fusion.16
  136.8 1.6 fusion.4
  138.4 0.0 reduce-scatter.11.cloned.1.call-update
  138.4 28.0 %reduce-scatter.11.cloned.1.call-done = f32[32,2048]{1,0:T(8,128)} async-done(((f32[128,2048]{1,0:T(8,128)}), f32[32,2048]{1,0:T(8,128)}) %reduce-scatter.11.cloned.1.call-update) | async-done | bytes 262160 | tf_op jit(solution)/shard_map/reduce_scatter | solution.py:51
  166.4 1.0 convert_bitcast_fusion
  167.4 7.1 %all_to_all.39 = bf16[4,8,2048]{2,1,0:T(8,128)(2,1)S(1)} all-to-all(bf16[4,8,2048]{2,1,0:T(8,128)(2,1)S(1)} %convert_bitcast_fusion), channel_id=1, replica_groups=mesh['groups'=2,'tensor'=4,'dp'=4] {'dp'}, dimensions={0} | all-to-all | bytes 262144 | tf_op jit(solution)/shard_map/all_to_all | solution.py:52
  174.5 0.7 copy.14
  (4 shorter events, 0.0 us)
Async XLA Ops:
  6.5 130.3 %copy-start = (bf16[64,8192]{1,0:T(8,128)(2,1)S(1)}, bf16[64,8192]{1,0:T(8,128)(2,1)}, u32[]{:S(2)}) copy-start(bf16[64,8192]{1,0:T(8,128)(2,1)} %param.19) | copy-start | bytes 3145732
  6.5 47.9 %reduce-scatter.13.cloned.1.call-start = ((), (), s32[]{:S(2)}) async-start(), calls=%async_computation.9 | async-start | bytes 81920
  33.8 52.9 %reduce-scatter.7.cloned.1.call-start = ((), (), s32[]{:S(2)}) async-start(), calls=%async_computation.6 | async-start | bytes 2293760 | tf_op jit(solution)/shard_map/reduce_scatter | solution.py:27
  42.3 44.4 %copy-start.2 = (bf16[64,3584]{1,0:T(8,128)(2,1)S(1)}, bf16[64,3584]{1,0:T(8,128)(2,1)}, u32[]{:S(2)}) copy-start(bf16[64,3584]{1,0:T(8,128)(2,1)} %param.15) | copy-start | bytes 1376260
  42.3 76.6 %copy-start.3 = (bf16[64,3584]{1,0:T(8,128)(2,1)S(1)}, bf16[64,3584]{1,0:T(8,128)(2,1)}, u32[]{:S(2)}) copy-start(bf16[64,3584]{1,0:T(8,128)(2,1)} %param.17) | copy-start | bytes 1376260
  42.3 76.5 %reduce-scatter.9.cloned.1.call-start = ((), (), s32[]{:S(2)}) async-start(), calls=%async_computation.7 | async-start | bytes 2293760 | tf_op jit(solution)/shard_map/reduce_scatter | solution.py:27
  51.0 85.5 %copy-start.1 = (bf16[3584,64]{0,1:T(8,128)(2,1)S(1)}, bf16[3584,64]{0,1:T(8,128)(2,1)}, u32[]{:S(2)}) copy-start(bf16[3584,64]{0,1:T(8,128)(2,1)} %param.18) | copy-start | bytes 1376260
  51.0 115.4 %reduce-scatter.11.cloned.1.call-start = ((), (), s32[]{:S(2)}) async-start(), calls=%async_computation.8 | async-start | bytes 1310720 | tf_op jit(solution)/shard_map/reduce_scatter | solution.py:51
Sparse Core Ops, SparseCore 0:
  33.9 20.5 reduce-scatter.12
  57.0 29.6 reduce-scatter.6
  89.2 29.5 reduce-scatter.8
  138.5 27.8 reduce-scatter.10

commit v2 on v1

v2 whole, which is shorter than its diff:
```python
import functools

import jax
import jax.numpy as jnp
from jax import lax
from jax.experimental import pallas as pl
from jax.experimental.pallas import tpu as pltpu
from jax.sharding import PartitionSpec as P

adapter_scale_factor = 0.5
MESH = pl.DeviceIdType.MESH
SUM_LAG, ACT_LAG, FWD_LAG, DOWN_LAG = 1, 2, 3, 4
SLOTS = ACT_LAG + 1


def kernel(
    nt, nd, nc,
    tok, wg, wu, wd, ag, go, au, uo, di, do, out,
    xbuf, x, wgv, wuv, wdv, agv, auv, gov, uov, div, dov,
    lowp, lowr, lowb, part, send_a, recv_a, send_b, recv_b, hid, acc, dl,
    osend, orecv, fin,
    wsem, ssem, tok_s, tok_r, low_s, low_r, a_s, a_r, b_s, b_r,
    h_s, h_r, p_s, p_r, f_s, f_r, o_s, o_r, z_s, z_r,
):
    n = nt * nd
    half = nd // 2
    depth = wg.shape[0]
    chunk = wgv.shape[2]
    width = wd.shape[1]
    tok_dev = tok.shape[0]
    total_rows = n * tok_dev
    rows = total_rows // nd
    block = nd * tok_dev
    my_t = lax.axis_index("tensor")
    my_d = lax.axis_index("dp")
    me = my_t * nd + my_d
    my_j = lax.div(my_d, 2)
    my_b = lax.rem(my_d, 2)
    other_b = 1 - my_b
    mate = my_j * 2 + other_b

    small = [
        pltpu.make_async_copy(tok.at[:, pl.ds(pl.multiple_of(my_d * depth, 128), depth)], xbuf.at[me], ssem.at[0]),
        pltpu.make_async_copy(ag, agv, ssem.at[1]),
        pltpu.make_async_copy(au, auv, ssem.at[2]),
        pltpu.make_async_copy(do.at[:, pl.ds(pl.multiple_of(my_d * width, 128), width)], dov, ssem.at[3]),
    ]

    def cols(ref, c):
        return ref.at[:, c * chunk : (c + 1) * chunk]

    def rows_of(ref, c):
        return ref.at[c * chunk : (c + 1) * chunk, :]

    plan = (
        (wg, wgv, cols), (wu, wuv, cols), (go, gov, cols), (uo, uov, cols),
        (wd, wdv, rows_of), (di, div, rows_of),
    )

    def load(kind, static_c, c):
        src, dst, cut = plan[kind]
        return pltpu.make_async_copy(cut(src, static_c), dst.at[c], wsem.at[kind, c])

    for copy in small[:3]:
        copy.start()
    for c in range(nc):
        for kind in range(4):
            load(kind, c, c).start()
    small[3].start()
    for c in range(nc):
        for kind in range(4, 6):
            load(kind, c, c).start()

    barrier = pltpu.get_barrier_semaphore()

    def place(index):
        return {"tensor": lax.div(index, nd), "dp": lax.rem(index, nd)}

    def greet(k, carry):
        pl.semaphore_signal(
            barrier, inc=1, device_id=place(lax.rem(me + k, n)), device_id_type=MESH
        )
        return carry

    lax.fori_loop(1, n, greet, 0)
    pl.semaphore_wait(barrier, n - 1)

    def remote(src, dst, send_sem, recv_sem, device):
        return pltpu.make_async_remote_copy(
            src_ref=src, dst_ref=dst, send_sem=send_sem, recv_sem=recv_sem,
            device_id=device, device_id_type=MESH,
        )

    def tok_copy(k):
        index = lax.rem(me + k, n)
        first = pl.multiple_of(lax.rem(index, nd) * depth, 128)
        return remote(
            tok.at[:, pl.ds(first, depth)], xbuf.at[me],
            tok_s.at[k - 1], tok_r.at[k - 1], place(index),
        )

    def each(low, high, act):
        def step(k, carry):
            act(k)
            return carry

        lax.fori_loop(low, high, step, 0)

    each(1, n, lambda k: tok_copy(k).start())
    small[0].wait()
    each(1, n, lambda k: tok_copy(k).wait_recv())
    x[...] = xbuf[...].astype(jnp.float32).reshape(total_rows, depth).astype(jnp.bfloat16)

    small[1].wait()
    small[2].wait()
    for which, ref in ((0, agv), (1, auv)):
        low = jnp.dot(x[...], ref[...], preferred_element_type=jnp.float32)
        for d in range(nd):
            lowp[d, which] = low[d * rows : (d + 1) * rows]

    def low_copy(k):
        d = lax.rem(my_d + k, nd)
        return remote(
            lowp.at[d], lowr.at[k - 1], low_s.at[k - 1], low_r.at[k - 1],
            {"tensor": my_t, "dp": d},
        )

    for k in range(1, nd):
        low_copy(k).start()

    def at_dp(d):
        return {"tensor": my_t, "dp": d}

    def a_copy(c):
        return remote(send_a.at[c], recv_a.at[c], a_s.at[c], a_r.at[c], at_dp(mate))

    def ahead(k):
        return lax.rem(my_j + k, half)

    def behind(k):
        return lax.rem(my_j + half - k, half) * 2 + my_b

    def b_copy(c, k):
        return remote(
            send_b.at[c, k - 1], recv_b.at[c, k - 1],
            b_s.at[c, k - 1], b_r.at[c, k - 1], at_dp(ahead(k) * 2 + my_b),
        )

    def h_copy(c, k):
        return remote(
            hid.at[c, my_d], hid.at[c, my_d],
            h_s.at[c, k - 1], h_r.at[c, k - 1], at_dp(ahead(k) * 2 + my_b),
        )

    def p_copy(c):
        return remote(hid.at[c, my_d], hid.at[c, my_d], p_s.at[c], p_r.at[c], at_dp(mate))

    def f_copy(c, k):
        return remote(
            hid.at[c, behind(k)], hid.at[c, behind(k)],
            f_s.at[c, k - 1], f_r.at[c, k - 1], at_dp(mate),
        )

    def rows_at(d):
        return pl.ds(pl.multiple_of(d * rows, rows), rows)

    def up_part(c):
        load(0, 0, c).wait()
        load(1, 0, c).wait()
        slot = lax.rem(c, SLOTS)
        part[slot, 0] = jnp.dot(x[...], wgv[c], preferred_element_type=jnp.float32)
        part[slot, 1] = jnp.dot(x[...], wuv[c], preferred_element_type=jnp.float32)
        for j in range(half):
            for which in range(2):
                send_a[c, j, which] = part[slot, which, rows_at(2 * j + other_b), :].astype(jnp.bfloat16)
        a_copy(c).start()

    def pair_sum(c):
        a_copy(c).wait_recv()
        slot = lax.rem(c, SLOTS)
        for k in range(1, half):
            j = ahead(k)
            for which in range(2):
                send_b[c, k - 1, which] = (
                    part[slot, which, rows_at(2 * j + my_b), :]
                    + recv_a[c, j, which].astype(jnp.float32)
                ).astype(jnp.bfloat16)
            b_copy(c, k).start()

    def activate(c):
        @pl.when(c == 0)
        def _():
            for k in range(1, nd):
                low_copy(k).wait_recv()
            total = lowp[my_d]
            for k in range(1, nd):
                total = total + lowr[k - 1]
            lowb[...] = total.astype(jnp.bfloat16)

        load(2, 0, c).wait()
        load(3, 0, c).wait()
        slot = lax.rem(c, SLOTS)
        for k in range(1, half):
            b_copy(c, k).wait_recv()
        sums = []
        for which, ref in ((0, gov), (1, uov)):
            value = part[slot, which, rows_at(my_d), :] + recv_a[c, my_j, which].astype(jnp.float32)
            for k in range(1, half):
                value = value + recv_b[c, k - 1, which].astype(jnp.float32)
            value = value + adapter_scale_factor * jnp.dot(
                lowb[which], ref[c], preferred_element_type=jnp.float32
            )
            sums.append(value)
        gate, up = sums
        hid[c, my_d] = (gate / (1.0 + jnp.exp(-gate)) * up).astype(jnp.bfloat16)
        for k in range(1, half):
            h_copy(c, k).start()
        p_copy(c).start()

    def forward(c):
        for k in range(1, half):
            h_copy(c, k).wait_recv()
            f_copy(c, k).start()

    def down_part(c):
        load(4, 0, c).wait()
        load(5, 0, c).wait()
        p_copy(c).wait_recv()
        for k in range(1, half):
            f_copy(c, k).wait_recv()
        lhs = hid[c].reshape(total_rows, chunk)

        @pl.when(c == 0)
        def _():
            acc[...] = jnp.zeros_like(acc)
            dl[...] = jnp.zeros_like(dl)

        step = 512 if width % 512 == 0 else width
        for first in range(0, width, step):
            acc[:, first : first + step] += jnp.dot(
                lhs, wdv[c, :, first : first + step], preferred_element_type=jnp.float32
            )
        dl[...] += jnp.dot(lhs, div[c], preferred_element_type=jnp.float32)

    stages = ((up_part, 0), (pair_sum, SUM_LAG), (activate, ACT_LAG), (forward, FWD_LAG), (down_part, DOWN_LAG))

    def turn(i, carry):
        for stage, lag in stages:
            c = i - lag
            pl.when(jnp.logical_and(c >= 0, c < nc))(functools.partial(stage, c))
        return carry

    lax.fori_loop(0, nc + DOWN_LAG, turn, 0)

    small[3].wait()
    low = dl[...]
    high = low.astype(jnp.bfloat16)
    rest = low - high.astype(jnp.float32)
    middle = rest.astype(jnp.bfloat16)
    last = (rest - middle.astype(jnp.float32)).astype(jnp.bfloat16)
    step = 512 if width % 512 == 0 else width
    for first in range(0, width, step):
        maps = dov[:, first : first + step]
        acc[:, first : first + step] += adapter_scale_factor * (
            jnp.dot(high, maps, preferred_element_type=jnp.float32)
            + (
                jnp.dot(middle, maps, preferred_element_type=jnp.float32)
                + jnp.dot(last, maps, preferred_element_type=jnp.float32)
            )
        )

    def block_at(t):
        return pl.ds(pl.multiple_of(t * block, block), block)

    def o_copy(k):
        t = lax.rem(my_t + k, nt)
        return remote(
            osend.at[k - 1], orecv.at[k - 1], o_s.at[k - 1], o_r.at[k - 1],
            {"tensor": t, "dp": my_d},
        )

    def o_send(k):
        osend[k - 1] = acc[block_at(lax.rem(my_t + k, nt)), :].astype(jnp.bfloat16)
        o_copy(k).start()

    each(1, nt, o_send)

    def o_take(k):
        o_copy(k).wait_recv()
        acc[block_at(my_t), :] += orecv[k - 1].astype(jnp.float32)

    each(1, nt, o_take)
    fin[...] = acc[block_at(my_t), :].reshape(nd, tok_dev, width).astype(jnp.bfloat16)
    mine = pl.ds(pl.multiple_of(my_d * width, 128), width)

    def z_copy(k):
        d = lax.rem(my_d + k, nd)
        return remote(fin.at[d], out.at[:, mine], z_s.at[k - 1], z_r.at[k - 1], at_dp(d))

    def z_wait(k):
        d = lax.rem(my_d + nd - k, nd)
        place_of = pl.ds(pl.multiple_of(d * width, 128), width)
        remote(fin.at[d], out.at[:, place_of], z_s.at[k - 1], z_r.at[k - 1], at_dp(d)).wait_recv()

    for k in range(1, nd):
        z_copy(k).start()
    out[:, mine] = fin[my_d]

    each(1, n, lambda k: tok_copy(k).wait_send())
    for k in range(1, nd):
        low_copy(k).wait_send()

    def drain(c, carry):
        a_copy(c).wait_send()
        p_copy(c).wait_send()
        for k in range(1, half):
            b_copy(c, k).wait_send()
            h_copy(c, k).wait_send()
            f_copy(c, k).wait_send()
        return carry

    lax.fori_loop(0, nc, drain, 0)
    each(1, nt, lambda k: o_copy(k).wait_send())
    for k in range(1, nd):
        z_wait(k)
        z_copy(k).wait_send()


def body(tok, wg, wu, wd, ag, go, au, uo, di, do):
    nt = lax.axis_size("tensor")
    nd = lax.axis_size("dp")
    n = nt * nd
    half = nd // 2
    tok_dev = tok.shape[0]
    depth, hidden = wg.shape
    width = wd.shape[1]
    rank = ag.shape[1]
    chunk = 512 if hidden % 512 == 0 else hidden
    nc = hidden // chunk
    total = n * tok_dev
    rows = total // nd
    block = nd * tok_dev
    far = half - 1
    bf, f32 = jnp.bfloat16, jnp.float32
    vm, dma = pltpu.VMEM, pltpu.SemaphoreType.DMA
    scratch = [
        vm((n, tok_dev, depth), bf), vm((total, depth), bf),
        vm((nc, depth, chunk), bf), vm((nc, depth, chunk), bf), vm((nc, chunk, width), bf),
        vm((depth, rank), bf), vm((depth, rank), bf),
        vm((nc, rank, chunk), bf), vm((nc, rank, chunk), bf), vm((nc, chunk, rank), bf),
        vm((rank, width), bf),
        vm((nd, 2, rows, rank), f32), vm((nd - 1, 2, rows, rank), f32), vm((2, rows, rank), bf),
        vm((SLOTS, 2, total, chunk), f32),
        vm((nc, half, 2, rows, chunk), bf), vm((nc, half, 2, rows, chunk), bf),
        vm((nc, far, 2, rows, chunk), bf), vm((nc, far, 2, rows, chunk), bf),
        vm((nc, nd, rows, chunk), bf),
        vm((total, width), f32), vm((total, rank), f32),
        vm((nt - 1, block, width), bf), vm((nt - 1, block, width), bf), vm((nd, tok_dev, width), bf),
        dma((6, nc)), dma((4,)), dma((n - 1,)), dma((n - 1,)), dma((nd - 1,)), dma((nd - 1,)),
        dma((nc,)), dma((nc,)), dma((nc, far)), dma((nc, far)),
        dma((nc, far)), dma((nc, far)), dma((nc,)), dma((nc,)), dma((nc, far)), dma((nc, far)),
        dma((nt - 1,)), dma((nt - 1,)), dma((nd - 1,)), dma((nd - 1,)),
    ]
    return pl.pallas_call(
        functools.partial(kernel, nt, nd, nc),
        out_shape=jax.ShapeDtypeStruct((tok_dev, width * nd), bf),
        in_specs=[pl.BlockSpec(memory_space=pl.ANY)] * 10,
        out_specs=pl.BlockSpec(memory_space=pltpu.VMEM),
        scratch_shapes=scratch,
        compiler_params=pltpu.CompilerParams(
            collective_id=0, has_side_effects=True, vmem_limit_bytes=67043328
        ),
    )(tok, wg, wu, wd, ag, go, au, uo, di, do)


def solution(mesh):
    placed = (
        P(("groups", "tensor", "dp"), None),
        P("dp", "tensor"),
        P("dp", "tensor"),
        P("tensor", "dp"),
        P(("groups", "dp"), None),
        P(None, ("groups", "tensor")),
        P(("groups", "dp"), None),
        P(None, ("groups", "tensor")),
        P(("groups", "tensor"), None),
        P(None, "groups"),
    )
    return jax.shard_map(
        body,
        mesh=mesh,
        in_specs=placed,
        out_specs=P(("groups", "tensor", "dp"), None),
        check_vma=False,
    )
```

time: 182 us -> 68.6 us (0.38)
  the two profiles are of different devices: /device:TPU:0 before, /device:TPU:29 now
where the time goes in v2:
time: 68.6 us; the launch traced here: 68.4 us
  Pallas kernels  60.6 us (88%)
  local copies, waits for them, and re-layouts  7.74 us (11%)
    pallas_call x1, Pallas kernels, body(): pl.pallas_call(functools.partial(kernel, nt, nd, nc), out_shape=jax.Shape...  60.6 us
    unnamed x4, local copies, waits for them, and re-layouts  7.74 us

profile of v2, /device:TPU:29, one launch (start us, length us, event | category | flops | bytes accessed | tf_op | source)
XLA Modules:
  0.0 68.4 jit_solution(12762873820462381493)
XLA Ops:
  0.0 2.0 %copy.11.ag = bf16[2048,64]{1,0:T(8,128)(2,1)} copy(bf16[2048,64]{0,1:T(8,128)(2,1)} %param.14) | data formatting | bytes 524288 | tf_op args[4]
  2.0 2.0 %copy.12.au = bf16[2048,64]{1,0:T(8,128)(2,1)} copy(bf16[2048,64]{0,1:T(8,128)(2,1)} %param.16) | data formatting | bytes 524288 | tf_op args[6]
  3.9 2.3 %copy.13.di = bf16[3584,64]{1,0:T(8,128)(2,1)} copy(bf16[3584,64]{0,1:T(8,128)(2,1)} %param.18) | data formatting | bytes 917504 | tf_op args[8]
  6.2 60.6 %shard_map.100 = bf16[8,8192]{1,0:T(8,128)(2,1)} custom-call(bf16[8,8192]{1,0:T(8,128)(2,1)} %tok.1, bf16[2048,3584]{1,0:T(8,128)(2,1)} %wg.1, bf16[2048,3584]{1,0:T(8,128)(2,1)} %wu.1, bf16[3584,2048]{1,0:T(8,128)(2,1)} %wd.1, bf16[2048,64]{1,0:T(8,128)(2,1)} %copy.11.ag, bf16[64,3584]{1,0:T(8,128)(2,1)} %go.1, bf16[2048,64]{1,0:T(8,128)(2,1)} %copy.12.au, ...), custom_call_target="tpu_custom_call" | custom-call | tf_op jit(solution)/shard_map/pallas_call | solution.py:364
  66.8 1.6 %copy.15 = bf16[8,8192]{1,0:T(8,128)(2,1)} copy(bf16[8,8192]{1,0:T(8,128)(2,1)} %shard_map.100) | data formatting | bytes 262144

commit v3 on v2

v3 whole, which is shorter than its diff:
```python
import functools

import jax
import jax.numpy as jnp
from jax import lax
from jax.experimental import pallas as pl
from jax.experimental.pallas import tpu as pltpu
from jax.sharding import PartitionSpec as P

adapter_scale_factor = 0.5
MESH = pl.DeviceIdType.MESH
HALVES = 2
SUM_LAG, ACT_LAG, FWD_LAG, DOWN_LAG = 2, 7, 12, 14


def dot_rows(a, b):
    return lax.dot_general(a, b, (((1,), (1,)), ((), ())), preferred_element_type=jnp.float32)


def kernel(
    nt, nd, nc,
    tok, wg, wu, wd, ag, go, au, uo, di, do, out,
    xbuf, x, wgv, wuv, wdv, agv, auv, gov, uov, div, dov,
    lowp, lowr, lowb, part, send_a, recv_a, send_b, recv_b, hid, acc, dl,
    osend, orecv, fin,
    wsem, ssem, tok_s, tok_r, low_s, low_r, a_s, a_r, b_s, b_r,
    h_s, h_r, p_s, p_r, f_s, f_r, o_s, o_r, z_s, z_r,
):
    n = nt * nd
    half = nd // 2
    depth = wg.shape[0]
    chunk = wgv.shape[2]
    width = wd.shape[1]
    tok_dev = tok.shape[0]
    total_rows = n * tok_dev
    side = total_rows // HALVES
    rows = side // nd
    owners = nd // HALVES
    block = owners * tok_dev
    my_t = lax.axis_index("tensor")
    my_d = lax.axis_index("dp")
    me = my_t * nd + my_d
    my_j = lax.div(my_d, 2)
    my_b = lax.rem(my_d, 2)
    other_b = 1 - my_b
    mate = my_j * 2 + other_b

    def slot_of(t, d):
        return (lax.div(d, owners) * nt + t) * owners + lax.rem(d, owners)

    my_slot = slot_of(my_t, my_d)

    small = [
        pltpu.make_async_copy(tok.at[:, pl.ds(pl.multiple_of(my_d * depth, 128), depth)], xbuf.at[my_slot], ssem.at[0]),
        pltpu.make_async_copy(ag, agv, ssem.at[1]),
        pltpu.make_async_copy(au, auv, ssem.at[2]),
        pltpu.make_async_copy(do.at[:, pl.ds(pl.multiple_of(my_d * width, 128), width)], dov, ssem.at[3]),
    ]

    def cols(ref, c):
        return ref.at[:, c * chunk : (c + 1) * chunk]

    def rows_of(ref, c):
        return ref.at[c * chunk : (c + 1) * chunk, :]

    plan = (
        (wg, wgv, cols), (wu, wuv, cols), (go, gov, cols), (uo, uov, cols),
        (wd, wdv, rows_of), (di, div, cols),
    )

    def load(kind, static_c, c):
        src, dst, cut = plan[kind]
        return pltpu.make_async_copy(cut(src, static_c), dst.at[c], wsem.at[kind, c])

    for copy in small[:3]:
        copy.start()
    for c in range(nc):
        for kind in range(4):
            load(kind, c, c).start()
    barrier = pltpu.get_barrier_semaphore()

    def place(index):
        return {"tensor": lax.div(index, nd), "dp": lax.rem(index, nd)}

    def greet(k, carry):
        pl.semaphore_signal(
            barrier, inc=1, device_id=place(lax.rem(me + k, n)), device_id_type=MESH
        )
        return carry

    lax.fori_loop(1, n, greet, 0)
    pl.semaphore_wait(barrier, n - 1)

    def remote(src, dst, send_sem, recv_sem, device):
        return pltpu.make_async_remote_copy(
            src_ref=src, dst_ref=dst, send_sem=send_sem, recv_sem=recv_sem,
            device_id=device, device_id_type=MESH,
        )

    def tok_copy(k):
        index = lax.rem(me + k, n)
        first = pl.multiple_of(lax.rem(index, nd) * depth, 128)
        return remote(
            tok.at[:, pl.ds(first, depth)], xbuf.at[my_slot],
            tok_s.at[k - 1], tok_r.at[k - 1], place(index),
        )

    def each(low, high, act):
        def step(k, carry):
            act(k)
            return carry

        lax.fori_loop(low, high, step, 0)

    each(1, n, lambda k: tok_copy(k).start())
    small[0].wait()
    each(1, n, lambda k: tok_copy(k).wait_recv())
    for c in range(nc):
        for kind in range(4, 6):
            load(kind, c, c).start()
    small[3].start()
    x[...] = xbuf[...].astype(jnp.float32).reshape(total_rows, depth).astype(jnp.bfloat16)

    small[1].wait()
    small[2].wait()
    for which, ref in ((0, agv), (1, auv)):
        low = dot_rows(x[...], ref[...])
        for d in range(nd):
            for s in range(HALVES):
                first = s * side + d * rows
                lowp[d, which, s] = low[first : first + rows]

    def low_copy(k):
        d = lax.rem(my_d + k, nd)
        return remote(
            lowp.at[d], lowr.at[k - 1], low_s.at[k - 1], low_r.at[k - 1],
            {"tensor": my_t, "dp": d},
        )

    for k in range(1, nd):
        low_copy(k).start()

    def at_dp(d):
        return {"tensor": my_t, "dp": d}

    def a_copy(c):
        return remote(send_a.at[c], recv_a.at[c], a_s.at[c], a_r.at[c], at_dp(mate))

    def ahead(k):
        return lax.rem(my_j + k, half)

    def behind(k):
        return lax.rem(my_j + half - k, half) * 2 + my_b

    def b_copy(c, k):
        return remote(
            send_b.at[c, k - 1], recv_b.at[c, k - 1],
            b_s.at[c, k - 1], b_r.at[c, k - 1], at_dp(ahead(k) * 2 + my_b),
        )

    def h_copy(c, k):
        return remote(
            hid.at[c, my_d], hid.at[c, my_d],
            h_s.at[c, k - 1], h_r.at[c, k - 1], at_dp(ahead(k) * 2 + my_b),
        )

    def p_copy(c):
        return remote(hid.at[c, my_d], hid.at[c, my_d], p_s.at[c], p_r.at[c], at_dp(mate))

    def f_copy(c, k):
        return remote(
            hid.at[c, behind(k)], hid.at[c, behind(k)],
            f_s.at[c, k - 1], f_r.at[c, k - 1], at_dp(mate),
        )

    def rows_at(s, d):
        return pl.ds(pl.multiple_of(s * side + d * rows, rows), rows)

    def up_part(c):
        load(0, 0, c).wait()
        load(1, 0, c).wait()
        part[c, 0] = jnp.dot(x[...], wgv[c], preferred_element_type=jnp.float32)
        part[c, 1] = jnp.dot(x[...], wuv[c], preferred_element_type=jnp.float32)
        for s in range(HALVES):
            for j in range(half):
                for which in range(2):
                    send_a[c, s, j, which] = part[c, which, rows_at(s, 2 * j + other_b), :].astype(
                        jnp.bfloat16
                    )
        a_copy(c).start()

    def pair_sum(q):
        s, c = lax.div(q, nc), lax.rem(q, nc)

        @pl.when(s == 0)
        def _():
            a_copy(c).wait_recv()

        for k in range(1, half):
            j = ahead(k)
            for which in range(2):
                send_b[q, k - 1, which] = (
                    part[c, which, rows_at(s, 2 * j + my_b), :]
                    + recv_a[c, s, j, which].astype(jnp.float32)
                ).astype(jnp.bfloat16)
            b_copy(q, k).start()

    def activate(q):
        s, c = lax.div(q, nc), lax.rem(q, nc)

        @pl.when(q == 0)
        def _():
            for k in range(1, nd):
                low_copy(k).wait_recv()
            total = lowp[my_d]
            for k in range(1, nd):
                total = total + lowr[k - 1]
            lowb[...] = total.astype(jnp.bfloat16)

        @pl.when(s == 0)
        def _():
            load(2, 0, c).wait()
            load(3, 0, c).wait()

        for k in range(1, half):
            b_copy(q, k).wait_recv()
        sums = []
        for which, ref in ((0, gov), (1, uov)):
            value = part[c, which, rows_at(s, my_d), :] + recv_a[c, s, my_j, which].astype(
                jnp.float32
            )
            for k in range(1, half):
                value = value + recv_b[q, k - 1, which].astype(jnp.float32)
            value = value + adapter_scale_factor * jnp.dot(
                lowb[which, s], ref[c], preferred_element_type=jnp.float32
            )
            sums.append(value)
        gate, up = sums
        hid[q, my_d] = (gate / (1.0 + jnp.exp(-gate)) * up).astype(jnp.bfloat16)
        for k in range(1, half):
            h_copy(q, k).start()
        p_copy(q).start()

    def forward(q):
        for k in range(1, half):
            h_copy(q, k).wait_recv()
            f_copy(q, k).start()

    step = 512 if width % 512 == 0 else width

    def down_part(q):
        s, c = lax.div(q, nc), lax.rem(q, nc)

        @pl.when(s == 0)
        def _():
            load(4, 0, c).wait()
            load(5, 0, c).wait()

        p_copy(q).wait_recv()
        for k in range(1, half):
            f_copy(q, k).wait_recv()
        lhs = hid[q].reshape(side, chunk)

        @pl.when(c == 0)
        def _():
            acc[s] = jnp.zeros((side, width), jnp.float32)
            dl[s] = jnp.zeros((side, dl.shape[2]), jnp.float32)

        for first in range(0, width, step):
            acc[s, :, first : first + step] += jnp.dot(
                lhs, wdv[c, :, first : first + step], preferred_element_type=jnp.float32
            )
        dl[s] += dot_rows(lhs, div[c])

        @pl.when(c == nc - 1)
        def _():
            finish(s)

    def finish(s):
        @pl.when(s == 0)
        def _():
            small[3].wait()

        low = dl[s]
        high = low.astype(jnp.bfloat16)
        rest = low - high.astype(jnp.float32)
        middle = rest.astype(jnp.bfloat16)
        last = (rest - middle.astype(jnp.float32)).astype(jnp.bfloat16)
        for first in range(0, width, step):
            maps = dov[:, first : first + step]
            acc[s, :, first : first + step] += adapter_scale_factor * (
                jnp.dot(high, maps, preferred_element_type=jnp.float32)
                + (
                    jnp.dot(middle, maps, preferred_element_type=jnp.float32)
                    + jnp.dot(last, maps, preferred_element_type=jnp.float32)
                )
            )

        def o_send(k):
            osend[s, k - 1] = acc[s, block_at(lax.rem(my_t + k, nt)), :].astype(jnp.bfloat16)
            o_copy(s, k).start()

        each(1, nt, o_send)

    def block_at(t):
        return pl.ds(pl.multiple_of(t * block, block), block)

    def o_copy(s, k):
        t = lax.rem(my_t + k, nt)
        return remote(
            osend.at[s, k - 1], orecv.at[s, k - 1], o_s.at[s, k - 1], o_r.at[s, k - 1],
            {"tensor": t, "dp": my_d},
        )

    mine = pl.ds(pl.multiple_of(my_d * width, 128), width)

    def z_copy(k):
        at = lax.rem(my_d + k, nd)
        return remote(
            fin.at[at], out.at[:, mine], z_s.at[k - 1], z_r.at[k - 1], at_dp(at)
        )

    stages = ((up_part, 0), (pair_sum, SUM_LAG), (activate, ACT_LAG), (forward, FWD_LAG), (down_part, DOWN_LAG))

    def turn(i, carry):
        for stage, lag in stages:
            c = i - lag
            count = nc if stage is up_part else HALVES * nc
            pl.when(jnp.logical_and(c >= 0, c < count))(functools.partial(stage, c))
        return carry

    lax.fori_loop(0, HALVES * nc + DOWN_LAG, turn, 0)

    for s in range(HALVES):
        def o_take(k, s=s):
            o_copy(s, k).wait_recv()
            acc[s, block_at(my_t), :] += orecv[s, k - 1].astype(jnp.float32)

        each(1, nt, o_take)
        fin[s * owners : (s + 1) * owners] = (
            acc[s, block_at(my_t), :].reshape(owners, tok_dev, width).astype(jnp.bfloat16)
        )
    for k in range(1, nd):
        z_copy(k).start()
    out[:, mine] = fin[my_d]

    each(1, n, lambda k: tok_copy(k).wait_send())
    for k in range(1, nd):
        low_copy(k).wait_send()

    def drain(q, carry):
        p_copy(q).wait_send()
        for k in range(1, half):
            b_copy(q, k).wait_send()
            h_copy(q, k).wait_send()
            f_copy(q, k).wait_send()
        return carry

    lax.fori_loop(0, HALVES * nc, drain, 0)
    each(0, nc, lambda c: a_copy(c).wait_send())
    for s in range(HALVES):
        each(1, nt, lambda k, s=s: o_copy(s, k).wait_send())

    def z_wait(k):
        d = lax.rem(my_d + nd - k, nd)
        place_of = pl.ds(pl.multiple_of(d * width, 128), width)
        remote(fin.at[d], out.at[:, place_of], z_s.at[k - 1], z_r.at[k - 1], at_dp(d)).wait_recv()

    for k in range(1, nd):
        z_wait(k)
        z_copy(k).wait_send()


def body(tok, wg, wu, wd, ag, go, au, uo, di, do):
    nt = lax.axis_size("tensor")
    nd = lax.axis_size("dp")
    n = nt * nd
    half = nd // 2
    tok_dev = tok.shape[0]
    depth, hidden = wg.shape
    width = wd.shape[1]
    rank = ag.shape[1]
    chunk = 512 if hidden % 512 == 0 else hidden
    nc = hidden // chunk
    total = n * tok_dev
    side = total // HALVES
    rows = side // nd
    block = nd // HALVES * tok_dev
    items = HALVES * nc
    far = half - 1
    bf, f32 = jnp.bfloat16, jnp.float32
    vm, dma = pltpu.VMEM, pltpu.SemaphoreType.DMA
    scratch = [
        vm((n, tok_dev, depth), bf), vm((total, depth), bf),
        vm((nc, depth, chunk), bf), vm((nc, depth, chunk), bf), vm((nc, chunk, width), bf),
        vm((rank, depth), bf), vm((rank, depth), bf),
        vm((nc, rank, chunk), bf), vm((nc, rank, chunk), bf), vm((nc, rank, chunk), bf),
        vm((rank, width), bf),
        vm((nd, 2, HALVES, rows, rank), f32), vm((nd - 1, 2, HALVES, rows, rank), f32), vm((2, HALVES, rows, rank), bf),
        vm((nc, 2, total, chunk), f32),
        vm((nc, HALVES, half, 2, rows, chunk), bf), vm((nc, HALVES, half, 2, rows, chunk), bf),
        vm((items, far, 2, rows, chunk), bf), vm((items, far, 2, rows, chunk), bf),
        vm((items, nd, rows, chunk), bf),
        vm((HALVES, side, width), f32), vm((HALVES, side, rank), f32),
        vm((HALVES, nt - 1, block, width), bf), vm((HALVES, nt - 1, block, width), bf),
        vm((nd, tok_dev, width), bf),
        dma((6, nc)), dma((4,)), dma((n - 1,)), dma((n - 1,)), dma((nd - 1,)), dma((nd - 1,)),
        dma((nc,)), dma((nc,)), dma((items, far)), dma((items, far)),
        dma((items, far)), dma((items, far)), dma((items,)), dma((items,)),
        dma((items, far)), dma((items, far)),
        dma((HALVES, nt - 1)), dma((HALVES, nt - 1)), dma((nd - 1,)), dma((nd - 1,)),
    ]
    return pl.pallas_call(
        functools.partial(kernel, nt, nd, nc),
        out_shape=jax.ShapeDtypeStruct((tok_dev, width * nd), bf),
        in_specs=[pl.BlockSpec(memory_space=pl.ANY)] * 10,
        out_specs=pl.BlockSpec(memory_space=pltpu.VMEM),
        scratch_shapes=scratch,
        compiler_params=pltpu.CompilerParams(
            collective_id=0, has_side_effects=True, vmem_limit_bytes=67043328
        ),
    )(tok, wg, wu, wd, ag.T, go, au.T, uo, di.T, do)


def solution(mesh):
    placed = (
        P(("groups", "tensor", "dp"), None),
        P("dp", "tensor"),
        P("dp", "tensor"),
        P("tensor", "dp"),
        P(("groups", "dp"), None),
        P(None, ("groups", "tensor")),
        P(("groups", "dp"), None),
        P(None, ("groups", "tensor")),
        P(("groups", "tensor"), None),
        P(None, "groups"),
    )
    return jax.shard_map(
        body,
        mesh=mesh,
        in_specs=placed,
        out_specs=P(("groups", "tensor", "dp"), None),
        check_vma=False,
    )
```

time: 68.6 us -> 55.1 us (0.80)
  the two profiles are of different devices: /device:TPU:29 before, /device:TPU:0 now
where the time goes in v3:
time: 55.1 us; the launch traced here: 55 us
  Pallas kernels  53.4 us (97%)
  local copies, waits for them, and re-layouts  1.57 us (3%)
    pallas_call x1, Pallas kernels, body(): pl.pallas_call(functools.partial(kernel, nt, nd, nc), out_shape=jax.Shape...  53.4 us
    unnamed x1, local copies, waits for them, and re-layouts  1.57 us

profile of v3, /device:TPU:0, one launch (start us, length us, event | category | flops | bytes accessed | tf_op | source)
XLA Modules:
  0.0 55.0 jit_solution(3615042925673430126)
XLA Ops:
  0.0 53.4 %shard_map.100 = bf16[8,8192]{1,0:T(8,128)(2,1)} custom-call(bf16[8,8192]{1,0:T(8,128)(2,1)} %tok.1, bf16[2048,3584]{1,0:T(8,128)(2,1)} %wg.1, bf16[2048,3584]{1,0:T(8,128)(2,1)} %wu.1, bf16[3584,2048]{1,0:T(8,128)(2,1)} %wd.1, bf16[64,2048]{1,0:T(8,128)(2,1)} %bitcast.4, bf16[64,3584]{1,0:T(8,128)(2,1)} %go.1, bf16[64,2048]{1,0:T(8,128)(2,1)} %bitcast.5, ...), custom_call_target="tpu_custom_call" | custom-call | tf_op jit(solution)/shard_map/pallas_call | solution.py:413
  53.4 1.6 %copy.12 = bf16[8,8192]{1,0:T(8,128)(2,1)} copy(bf16[8,8192]{1,0:T(8,128)(2,1)} %shard_map.100) | data formatting | bytes 262144

commit v4 on v3

--- a/solution.py
+++ b/solution.py
@@ -10,7 +10,7 @@
 adapter_scale_factor = 0.5
 MESH = pl.DeviceIdType.MESH
 HALVES = 2
-SUM_LAG, ACT_LAG, FWD_LAG, DOWN_LAG = 2, 7, 12, 14
+SUM_LAG, ACT_LAG, FWD_LAG, DOWN_LAG = 2, 8, 14, 16
 
 
 def dot_rows(a, b):

time: 55.1 us -> 55.1 us (level)
  no operation moved by 1% of the time
where the time goes in v4:
time: 55.1 us; the launch traced here: 54.9 us
  Pallas kernels  53.3 us (97%)
  local copies, waits for them, and re-layouts  1.57 us (3%)
    pallas_call x1, Pallas kernels, body(): pl.pallas_call(functools.partial(kernel, nt, nd, nc), out_shape=jax.Shape...  53.3 us
    unnamed x1, local copies, waits for them, and re-layouts  1.57 us

profile of v4, /device:TPU:0, one launch (start us, length us, event | category | flops | bytes accessed | tf_op | source)
XLA Modules:
  0.0 54.9 jit_solution(16621324913618417956)
XLA Ops:
  0.0 53.3 %shard_map.100 = bf16[8,8192]{1,0:T(8,128)(2,1)} custom-call(bf16[8,8192]{1,0:T(8,128)(2,1)} %tok.1, bf16[2048,3584]{1,0:T(8,128)(2,1)} %wg.1, bf16[2048,3584]{1,0:T(8,128)(2,1)} %wu.1, bf16[3584,2048]{1,0:T(8,128)(2,1)} %wd.1, bf16[64,2048]{1,0:T(8,128)(2,1)} %bitcast.4, bf16[64,3584]{1,0:T(8,128)(2,1)} %go.1, bf16[64,2048]{1,0:T(8,128)(2,1)} %bitcast.5, ...), custom_call_target="tpu_custom_call" | custom-call | tf_op jit(solution)/shard_map/pallas_call | solution.py:413
  53.3 1.6 %copy.12 = bf16[8,8192]{1,0:T(8,128)(2,1)} copy(bf16[8,8192]{1,0:T(8,128)(2,1)} %shard_map.100) | data formatting | bytes 262144
